TPU v7x, 256 devices: a whole 4x4x8 slice. The times are simulated.
256 devices in a mesh: req: 16 (over z, core), mp: 16 (over x, y).
Axes of the slice: x: 4, y: 4, z: 8, core: 2. Of those that a mesh axis runs over, the one named last changes fastest.
Arguments:
- tokens: bfloat16 [1568, 7168], P('req', 'mp'), may hold values from -6 to 6
- layernorm_scale: float32 [7168], replicated, may hold values from 0.5 to 1.5
- layernorm_bias: float32 [7168], replicated, may hold values from -3 to 3
- query_key_value_weight: bfloat16 [3, 7168, 6144], P(None, 'req', 'mp'), may hold values from -0.0625 to 0.0625
- query_key_value_bias: float32 [3, 6144], P(None, 'mp'), may hold values from -3 to 3
- adapter_down_weight: bfloat16 [64, 7168, 32], P('req', 'mp'), may hold values from -0.0625 to 0.0625
- adapter_up_weight: bfloat16 [64, 2, 16, 6144], P('req', None, None, 'mp'), may hold values from -1.5 to 1.5
- adapter_index_table: int32 [16, 5], P('req'), may hold values from 0 to 63
- prompt_length_list: int32 [48], P('req'), may hold values from 1 to 32, 960 in all
- cache: bfloat16 [32, 2048, 2, 6144], P('req', None, None, 'mp'), may hold values from -320 to 320, as said below
- cache_length_list: int32 [32], P('req'), may hold values from 1 to 2048, 20480 in all
- output_weight: bfloat16 [6144, 7168], P('mp', 'req'), may hold values from -0.078125 to 0.078125
- output_bias: float32 [7168], P('mp'), may hold values from -3 to 3
Outputs:
- layer_out: bfloat16 [1568, 7168], P('req', 'mp')
Inputs may be any that keep to these rules, and one draw needn't show every extreme that they name: Each prompt fills the first prompt_length_list rows of its slot of 32 rows. Live cache positions are the first cache_length_list of each slot. `cache`: entries mostly of order one, though rare keys may be larger.
All inputs are finite; a program needn't handle non-finite values. No bound on the sum of `prompt_length_list` or of `cache_length_list` on one device may be relied on, other than what follows from the above.
Results may differ from a plain program's by a relative error of at most 0.015.
Values may be sent and summed in bfloat16 or wider, within the bound.
A program may use at most 128 MiB of HBM per device.

v0:
```python
import jax
import jax.numpy as jnp
from jax import lax
from jax.sharding import PartitionSpec as P

HEAD_DIM = 128
ADAPTER_RANK = 16


def layer_norm(row_data, gain_vec, shift_vec):
    values = row_data.astype(jnp.float32)
    average = jnp.mean(values, axis=-1, keepdims=True)
    centred = values - average
    variance = jnp.mean(centred * centred, axis=-1, keepdims=True)
    scaled = centred * lax.rsqrt(variance + 1e-05)
    return (scaled * gain_vec + shift_vec).astype(jnp.bfloat16)


def on_device(
    tokens,
    layernorm_scale,
    layernorm_bias,
    query_key_value_weight,
    query_key_value_bias,
    adapter_down_weight,
    adapter_up_weight,
    adapter_index_table,
    prompt_length_list,
    cache,
    cache_length_list,
    output_weight,
    output_bias,
):
    rows_dev = tokens.shape[0]
    part_cols = tokens.shape[1]
    decode_count = cache.shape[0]
    slot_count = prompt_length_list.shape[0]
    prompt_rows = rows_dev - decode_count
    slot_len = prompt_rows // slot_count
    rank_size = ADAPTER_RANK
    head_count = query_key_value_weight.shape[2] // HEAD_DIM
    score_scale = HEAD_DIM ** (-0.5)
    gathered = lax.all_gather(tokens, "mp", axis=1, tiled=True)
    normed = layer_norm(gathered, layernorm_scale, layernorm_bias)
    column = lax.axis_index("mp")
    slice_m = lax.dynamic_slice_in_dim(normed, column * part_cols, part_cols, 1)
    spread = lax.all_to_all(normed, "req", split_axis=1, concat_axis=0, tiled=True)
    projected = lax.psum_scatter(
        jnp.einsum(
            "rd,cde->rce", spread, query_key_value_weight, preferred_element_type=jnp.float32
        ),
        "req",
        scatter_dimension=0,
        tiled=True,
    )
    projected = projected + query_key_value_bias[None]
    positions = jnp.arange(rows_dev)
    request_slot = jnp.where(
        positions < prompt_rows, positions // slot_len, slot_count + positions - prompt_rows
    )
    slot_match = request_slot[:, None] == jnp.arange(slot_count + decode_count)[None, :]
    row_adapter = jnp.sum(jnp.where(slot_match, adapter_index_table[0][None, :], 0), axis=1)
    adapter_on_device = adapter_down_weight.shape[0]
    owners = lax.axis_size("req")
    owner_row = row_adapter // adapter_on_device
    to_owner = owner_row[None, :] == jnp.arange(owners)[:, None]
    outgoing = jnp.where(to_owner[:, :, None], slice_m[None], jnp.zeros((), jnp.bfloat16))
    labels = jnp.where(to_owner, (row_adapter - owner_row * adapter_on_device)[None, :], -1)
    received_rows = lax.all_to_all(outgoing, "req", split_axis=0, concat_axis=0, tiled=True)
    arrived_labels = lax.all_to_all(labels, "req", split_axis=0, concat_axis=0, tiled=True)
    sources, items = arrived_labels.shape
    selection_mask = (
        arrived_labels[:, :, None] == jnp.arange(adapter_on_device)[None, None, :]
    ).astype(jnp.float32)
    adapter_wise_sums = jnp.einsum(
        "yju,ouv->yjov", received_rows, adapter_down_weight, preferred_element_type=jnp.float32
    )
    reduced_rank_rows = jnp.einsum("ogf,ogft->ogt", selection_mask, adapter_wise_sums)
    reduced_rank_rows = lax.psum(reduced_rank_rows, "mp").astype(jnp.bfloat16)
    broadcast_rank_rows = selection_mask.astype(jnp.bfloat16)[
        :, :, :, None, None
    ] * reduced_rank_rows.reshape(sources, items, 1, 2, rank_size)
    corrections = jnp.einsum(
        "pqwgd,wgdx->pqgx",
        broadcast_rank_rows,
        adapter_up_weight,
        preferred_element_type=jnp.float32,
    ).astype(jnp.bfloat16)
    returned = lax.all_to_all(corrections, "req", split_axis=0, concat_axis=0, tiled=True)
    adapter_delta = jnp.sum(returned.astype(jnp.float32), axis=0)
    queries = (projected[:, 0] + adapter_delta[:, 0]).astype(jnp.bfloat16)
    keys_new = projected[:, 1].astype(jnp.bfloat16)
    values_new = (projected[:, 2] + adapter_delta[:, 1]).astype(jnp.bfloat16)
    prompt_q = queries[:prompt_rows].reshape(slot_count, slot_len, head_count, HEAD_DIM)
    prompt_k = keys_new[:prompt_rows].reshape(slot_count, slot_len, head_count, HEAD_DIM)
    prompt_v = values_new[:prompt_rows].reshape(slot_count, slot_len, head_count, HEAD_DIM)
    scores = (
        jnp.einsum("sihd,sjhd->shij", prompt_q, prompt_k, preferred_element_type=jnp.float32)
        * score_scale
    )
    causal = jnp.arange(slot_len)[None, :] <= jnp.arange(slot_len)[:, None]
    scores = jnp.where(causal[None, None], scores, -1e30)
    highest = jnp.max(scores, axis=3, keepdims=True)
    weights = jnp.where(causal[None, None], jnp.exp(scores - highest), 0.0)
    weights = (weights / jnp.sum(weights, axis=3, keepdims=True)).astype(jnp.bfloat16)
    prompt_out = jnp.einsum(
        "shij,sjhd->sihd", weights, prompt_v, preferred_element_type=jnp.float32
    )
    active = jnp.arange(slot_len)[None, :] < prompt_length_list[:, None]
    prompt_out = (
        jnp.where(active[:, :, None, None], prompt_out, 0.0)
        .astype(jnp.bfloat16)
        .reshape(prompt_rows, -1)
    )
    cache_len = cache.shape[1]
    decode_q = queries[prompt_rows:].reshape(decode_count, head_count, HEAD_DIM)
    decode_k = keys_new[prompt_rows:].reshape(decode_count, head_count, HEAD_DIM)
    decode_v = values_new[prompt_rows:].reshape(decode_count, head_count, HEAD_DIM)
    keys_old = cache[:, :, 0].reshape(decode_count, cache_len, head_count, HEAD_DIM)
    values_old = cache[:, :, 1].reshape(decode_count, cache_len, head_count, HEAD_DIM)
    cache_scores = (
        jnp.einsum("dhe,dthe->dht", decode_q, keys_old, preferred_element_type=jnp.float32)
        * score_scale
    )
    live_cache = jnp.arange(cache_len)[None, None, :] < cache_length_list[:, None, None]
    cache_scores = jnp.where(live_cache, cache_scores, -1e30)
    self_score = (
        jnp.einsum("dhe,dhe->dh", decode_q, decode_k, preferred_element_type=jnp.float32)
        * score_scale
    )
    row_top = jnp.maximum(jnp.max(cache_scores, axis=2), self_score)
    cache_weights = jnp.where(live_cache, jnp.exp(cache_scores - row_top[:, :, None]), 0.0)
    self_weight = jnp.exp(self_score - row_top)
    totals = jnp.sum(cache_weights, axis=2) + self_weight
    cache_weights = (cache_weights / totals[:, :, None]).astype(jnp.bfloat16)
    self_weight = (self_weight / totals).astype(jnp.bfloat16)
    decode_out = jnp.einsum(
        "dht,dthe->dhe", cache_weights, values_old, preferred_element_type=jnp.float32
    )
    decode_out = decode_out + self_weight.astype(jnp.float32)[:, :, None] * decode_v.astype(
        jnp.float32
    )
    decode_out = decode_out.astype(jnp.bfloat16).reshape(decode_count, -1)
    attended = jnp.concatenate([prompt_out, decode_out], axis=0)
    mixed = jnp.dot(
        attended,
        lax.all_gather(output_weight, "req", axis=1, tiled=True),
        preferred_element_type=jnp.float32,
    )
    summed = lax.psum_scatter(
        mixed.astype(jnp.bfloat16), "mp", scatter_dimension=1, tiled=True
    ).astype(jnp.float32)
    return (tokens.astype(jnp.float32) + summed + output_bias[None]).astype(jnp.bfloat16)


def solution(mesh):
    placed = (
        P("req", "mp"),
        P(),
        P(),
        P(None, "req", "mp"),
        P(None, "mp"),
        P("req", "mp", None),
        P("req", None, None, "mp"),
        P("req", None),
        P("req"),
        P("req", None, None, "mp"),
        P("req"),
        P("mp", "req"),
        P("mp"),
    )
    return jax.shard_map(
        on_device, mesh=mesh, in_specs=placed, out_specs=P("req", "mp"), check_vma=False
    )
```

profile of v0, /device:TPU:32, one launch (start us, length us, event | category | flops | bytes accessed | tf_op | source)
XLA Modules:
  0.0 485.0 jit_solution(15356733694840684768)
XLA Ops:
  7.3 54.4 %all-gather.6.cloned.1.call-done = bf16[16,448,98]{1,2,0:T(8,128)(2,1)} async-done(((bf16[1,448,98]{1,2,0:T(8,128)(2,1)}), bf16[16,448,98]{1,2,0:T(8,128)(2,1)}) %all-gather.6.cloned.1.call-update) | async-done | bytes 1404944 | tf_op jit(solution)/shard_map/all_gather | solution.py:43
  61.7 3.6 copy.59
  65.3 4.7 reshape.248
  70.4 2.5 multiply_reduce_fusion
  72.9 1.7 fusion.1
  74.6 3.2 all_to_all.24
  78.7 48.4 %all_to_all.35 = bf16[98,16,448]{2,0,1:T(8,128)(2,1)S(1)} all-to-all(bf16[98,16,448]{2,0,1:T(8,128)(2,1)S(1)} %copy.60), channel_id=1, replica_groups=mesh['req'=16,'mp'=16] {'req'}, dimensions={1} | all-to-all | bytes 2809856 | tf_op jit(solution)/shard_map/all_to_all | solution.py:47
  127.1 1.7 all_to_all.27
  128.8 6.6 %fusion.5 = f32[1568,3,384]{2,0,1:T(8,128)} fusion(bf16[3,448,384]{2,1,0:T(8,128)(2,1)S(1)} %copy-done, bf16[1568,448]{1,0:T(8,128)(2,1)} %all_to_all.27), kind=kOutput, calls=%fused_computation.11 | convolution fusion | flops 1618477056 | bytes 9662464 | tf_op jit(solution)/shard_map/rd,cde->rce/dot_general | solution.py:49
  136.8 4.7 all-to-all-start.1
  141.5 1.0 constant_dynamic-slice_fusion.1
  142.5 1.5 broadcast_select_fusion
  144.0 3.6 all-to-all-done.1
  147.7 5.0 %all-to-all-start.2 = ((bf16[16,98,448]{2,1,0:T(8,128)(2,1)}), bf16[16,98,448]{2,1,0:T(8,128)(2,1)S(1)}, u32[]{:S(2)}, u32[]{:S(2)}) async-start(bf16[16,98,448]{2,1,0:T(8,128)(2,1)} %broadcast_select_fusion), calls=%async_computation.2 | async-start | bytes 3407872 | tf_op jit(solution)/shard_map/all_to_all | solution.py:69
  153.5 46.5 %all-to-all-done.2 = bf16[16,98,448]{2,1,0:T(8,128)(2,1)S(1)} async-done(((bf16[16,98,448]{2,1,0:T(8,128)(2,1)}), bf16[16,98,448]{2,1,0:T(8,128)(2,1)S(1)}, u32[]{:S(2)}, u32[]{:S(2)}) %all-to-all-start.2) | async-done | bytes 1404960 | tf_op jit(solution)/shard_map/all_to_all | solution.py:69
  200.7 74.7 %all-reduce.5 = bf16[16,98,32]{1,2,0:T(8,128)(2,1)S(1)} all-reduce(f32[16,98,32]{1,2,0:T(8,128)S(1)} %fusion.10), channel_id=1, replica_groups=mesh['req'=16,'mp'=16] {'mp'}, use_global_device_ids=true, to_apply=%region_4.5 | all-reduce | flops 50176 | bytes 301056 | tf_op jit(solution)/shard_map/psum | solution.py:79
  276.3 4.0 copy.65
  280.3 7.5 %all-to-all-start.3 = ((bf16[16,98,2,384]{3,2,1,0:T(2,128)(2,1)}), bf16[16,98,2,384]{3,2,1,0:T(2,128)(2,1)S(1)}, u32[]{:S(2)}, u32[]{:S(2)}) async-start(bf16[16,98,2,384]{3,2,1,0:T(2,128)(2,1)} %copy.65), calls=%async_computation.3 | async-start | bytes 4816896 | tf_op jit(solution)/shard_map/all_to_all | solution.py:89
  287.8 13.8 %fusion.54 = (bf16[2,2048,1,384]{3,2,1,0:T(2,128)(2,1)}, bf16[2,2048,1,384]{3,2,1,0:T(2,128)(2,1)}) fusion(bf16[2,2048,2,384]{3,2,1,0:T(2,128)(2,1)} %param.22), kind=kLoop, calls=%fused_computation.103 | loop fusion | bytes 12582912 | tf_op jit(solution)/shard_map/slice | solution.py:119
  301.6 15.3 %copy.100 = bf16[2,2048,1,384]{1,3,0,2:T(8,128)(2,1)} copy(bf16[2,2048,1,384]{3,2,1,0:T(2,128)(2,1)} %get-tuple-element.9) | data formatting | bytes 6291456
  316.9 15.4 %copy.101 = bf16[2,2048,1,384]{1,3,0,2:T(8,128)(2,1)} copy(bf16[2,2048,1,384]{3,2,1,0:T(2,128)(2,1)} %get-tuple-element.10) | data formatting | bytes 6291456
  333.8 1.1 constant_dynamic-slice_fusion
  334.9 1.1 fusion.52
  336.5 8.8 %all-to-all-done.3 = bf16[16,98,2,384]{3,2,1,0:T(2,128)(2,1)S(1)} async-done(((bf16[16,98,2,384]{3,2,1,0:T(2,128)(2,1)}), bf16[16,98,2,384]{3,2,1,0:T(2,128)(2,1)S(1)}, u32[]{:S(2)}, u32[]{:S(2)}) %all-to-all-start.3) | async-done | bytes 2408480 | tf_op jit(solution)/shard_map/all_to_all | solution.py:89
  345.3 2.0 convert_reduce_fusion
  349.3 2.4 fusion.43
  352.3 2.8 fusion.34
  355.2 36.3 %all-gather.4.cloned.1.call-done = bf16[384,7168]{0,1:T(8,128)(2,1)} async-done(((bf16[384,448]{0,1:T(8,128)(2,1)}), bf16[384,7168]{0,1:T(8,128)(2,1)}) %all-gather.4.cloned.1.call-update) | async-done | bytes 5505040 | tf_op jit(solution)/shard_map/all_gather | solution.py:147
  391.5 5.0 %convolution_convert_fusion = bf16[98,7168]{1,0:T(8,128)(2,1)S(1)} fusion(bf16[384,7168]{0,1:T(8,128)(2,1)} %all-gather.4.cloned.1.call-done, bf16[2,384]{1,0:T(2,128)(2,1)S(1)} %bitcast.94, bf16[96,384]{1,0:T(8,128)(2,1)S(1)} %bitcast.91), kind=kOutput, calls=%fused_computation.1 | convolution fusion | flops 540345344 | bytes 6985216 | tf_op jit(solution)/shard_map/dot_general | solution.py:145
  396.5 2.4 copy.98
  398.9 77.8 %reduce-scatter.5.cloned.1.call-done = bf16[448,98]{1,0:T(8,128)(2,1)} async-done(((bf16[7168,98]{1,0:T(8,128)(2,1)}), bf16[448,98]{1,0:T(8,128)(2,1)}) %reduce-scatter.5.cloned.1.call-update) | async-done | bytes 87824
  476.8 1.0 copy.99
  (85 shorter events, 10.4 us)
Async XLA Ops:
  6.5 122.3 %copy-start = (bf16[3,448,384]{2,1,0:T(8,128)(2,1)S(1)}, bf16[3,448,384]{2,1,0:T(8,128)(2,1)}, u32[]{:S(2)}) copy-start(bf16[3,448,384]{2,1,0:T(8,128)(2,1)} %param.16) | copy-start | bytes 3096580
  6.5 55.1 %all-gather.6.cloned.1.call-start = ((), (), s32[]{:S(2)}) async-start(), calls=%async_computation.6 | async-start | bytes 1810432 | tf_op jit(solution)/shard_map/all_gather | solution.py:43
  7.3 326.6 %all-reduce.4.cloned.1.call-start = ((), (), s32[]{:S(2)}) async-start(), calls=%async_computation.8 | async-start | bytes 14450688
  65.3 4.7 copy-start.3
  70.0 2.9 copy-start.2
  70.0 2.9 copy-start.7
  70.0 2.9 copy-start.8
  135.5 0.7 copy-start.13
  135.5 64.4 %copy-start.12 = (bf16[4,448,32]{1,2,0:T(8,128)(2,1)S(1)}, bf16[4,448,32]{1,2,0:T(8,128)(2,1)}, u32[]{:S(2)}) copy-start(bf16[4,448,32]{1,2,0:T(8,128)(2,1)} %param.18) | copy-start | bytes 344068
  136.8 10.8 %all-to-all-start.1 = ((s32[16,1,98]{2,1,0:T(1,128)}), s32[16,1,98]{2,1,0:T(1,128)S(1)}, u32[]{:S(2)}, u32[]{:S(2)}) async-start(s32[16,1,98]{2,1,0:T(1,128)} %compare_select_fusion), calls=%async_computation.1 | async-start | bytes 16384 | tf_op jit(solution)/shard_map/all_to_all | solution.py:70
  144.0 131.3 %copy-start.6 = (bf16[4,2,16,384]{3,2,1,0:T(8,128)(2,1)S(1)}, bf16[4,2,16,384]{3,2,1,0:T(8,128)(2,1)}, u32[]{:S(2)}) copy-start(bf16[4,2,16,384]{3,2,1,0:T(8,128)(2,1)} %param.19) | copy-start | bytes 294916
  147.7 52.2 %all-to-all-start.2 = ((bf16[16,98,448]{2,1,0:T(8,128)(2,1)}), bf16[16,98,448]{2,1,0:T(8,128)(2,1)S(1)}, u32[]{:S(2)}, u32[]{:S(2)}) async-start(bf16[16,98,448]{2,1,0:T(8,128)(2,1)} %broadcast_select_fusion), calls=%async_computation.2 | async-start | bytes 3407872 | tf_op jit(solution)/shard_map/all_to_all | solution.py:69
  152.7 238.8 %all-gather.4.cloned.1.call-start = ((), (), s32[]{:S(2)}) async-start(), calls=%async_computation.5 | async-start | bytes 5849088 | tf_op jit(solution)/shard_map/all_gather | solution.py:147
  280.3 65.1 %all-to-all-start.3 = ((bf16[16,98,2,384]{3,2,1,0:T(2,128)(2,1)}), bf16[16,98,2,384]{3,2,1,0:T(2,128)(2,1)S(1)}, u32[]{:S(2)}, u32[]{:S(2)}) async-start(bf16[16,98,2,384]{3,2,1,0:T(2,128)(2,1)} %copy.65), calls=%async_computation.3 | async-start | bytes 4816896 | tf_op jit(solution)/shard_map/all_to_all | solution.py:89
  287.8 189.0 %reduce-scatter.5.cloned.1.call-start = ((), (), s32[]{:S(2)}) async-start(), calls=%async_computation.7 | async-start | bytes 1949696
  316.9 15.4 %copy-start.15 = (u32[256]{0:T(256)S(1)}, u32[256]{0:T(256)}, u32[]{:S(2)}) copy-start(u32[256]{0:T(256)} %constant.76) | copy-start | bytes 3076
  316.9 16.7 %copy-start.14 = (s32[3]{0:T(128)S(1)}, s32[3]{0:T(128)}, u32[]{:S(2)}) copy-start(s32[3]{0:T(128)} %param.21) | copy-start | bytes 40
  316.9 16.8 %copy-start.11 = (s32[2]{0:T(128)S(1)}, s32[2]{0:T(128)}, u32[]{:S(2)}) copy-start(s32[2]{0:T(128)} %param.23) | copy-start | bytes 28
  316.9 18.0 %copy-start.9 = (f32[3,384]{1,0:T(4,128)S(1)}, f32[3,384]{1,0:T(4,128)}, u32[]{:S(2)}) copy-start(f32[3,384]{1,0:T(4,128)} %param.17) | copy-start | bytes 13828
  336.0 11.4 %copy-start.4 = (f32[98,3,384]{2,1,0:T(4,128)S(1)}, f32[98,3,384]{2,1,0:T(4,128)}, u32[]{:S(2)}) copy-start(f32[98,3,384]{2,1,0:T(4,128)} %get-tuple-element.14) | copy-start | bytes 1354756
  391.5 87.0 %copy-start.1 = (bf16[3,448,384]{2,1,0:T(8,128)(2,1)S(1)}, bf16[3,448,384]{2,1,0:T(8,128)(2,1)}, u32[]{:S(2)}) copy-start(bf16[3,448,384]{2,1,0:T(8,128)(2,1)} %param.16) | copy-start | bytes 3096580
  396.5 81.3 %copy-start.5 = (bf16[98,448]{1,0:T(8,128)(2,1)S(1)}, bf16[98,448]{1,0:T(8,128)(2,1)}, u32[]{:S(2)}) copy-start(bf16[98,448]{1,0:T(8,128)(2,1)} %param.13) | copy-start | bytes 263428
  396.5 81.3 %copy-start.10 = (f32[448]{0:T(512)S(1)}, f32[448]{0:T(512)}, u32[]{:S(2)}) copy-start(f32[448]{0:T(512)} %param.25) | copy-start | bytes 5380
Sparse Core Ops, SparseCore 0:
  9.8 51.8 all-gather.5
  135.6 178.3 all-reduce.3
  315.9 75.5 all-gather.3
  399.1 77.6 reduce-scatter.4
where the time goes:
time: 486 us; the launch traced here: 485 us
  waiting for transfers between devices  229 us (47%)
  blocking collectives  123 us (25%)
  local copies, waits for them, and re-layouts  71 us (15%)
  matrix products  18.9 us (4%)
  starting transfers between devices  17.3 us (4%)
  between operations  14.1 us (3%)
  other arithmetic  11.7 us (2%)
    unnamed x6, waiting for transfers between devices  79.3 us
    psum x1, blocking collectives, on_device(): reduced_rank_rows = lax.psum(reduced_rank_rows, 'mp').astype(jnp.bfloat16)  74.7 us
    all_gather x1, waiting for transfers between devices, on_device(): gathered = lax.all_gather(tokens, 'mp', axis=1, tiled=True)  54.4 us
    all_to_all x1, blocking collectives, on_device(): lax.all_to_all(normed, 'req', split_axis=1, concat_axis=0, tiled=True)  48.4 us
    all_to_all x1, waiting for transfers between devices, on_device(): lax.all_to_all(outgoing, 'req', split_axis=0, concat_axis=0, tiled=True)  46.5 us
    unnamed x40, local copies, waits for them, and re-layouts  36.5 us
    all_gather x1, waiting for transfers between devices, on_device(): lax.all_gather(output_weight, 'req', axis=1, tiled=True)  36.3 us
    slice x1, local copies, waits for them, and re-layouts, on_device(): cache[:, :, 0].reshape(decode_count, cache_len, head_count, HEAD_DIM)  13.8 us
  transfers between devices with their start and end apart: 7, of which 6 were waited for; matrix products, arithmetic and copies ran while one was open for 14% of the time, Pallas kernels for 0%

commit v1 on v0

--- a/solution.py
+++ b/solution.py
@@ -5,6 +5,30 @@
 
 HEAD_DIM = 128
 ADAPTER_RANK = 16
+
+
+def write_sites_in(u, mesh_name, row_dim):
+    now, outer, opened = (lax.axis_size(mesh_name), lax.axis_index(mesh_name), u.shape[row_dim])
+    g_now = lax.dynamic_update_slice_in_dim(
+        jnp.zeros([s * now if dev_i == row_dim else s for dev_i, s in enumerate(u.shape)], u.dtype),
+        u,
+        outer * opened,
+        axis=row_dim,
+    )
+    right_arr = r1 = u
+    for tick in range(1, now // 2 + 1):
+        right_arr = lax.ppermute(
+            right_arr, mesh_name, [(dev_i, (dev_i + 1) % now) for dev_i in range(now)]
+        )
+        g_now = lax.dynamic_update_slice_in_dim(
+            g_now, right_arr, (outer - tick) % now * opened, axis=row_dim
+        )
+        if 2 * tick < now:
+            r1 = lax.ppermute(r1, mesh_name, [(dev_i, (dev_i - 1) % now) for dev_i in range(now)])
+            g_now = lax.dynamic_update_slice_in_dim(
+                g_now, r1, (outer + tick) % now * opened, axis=row_dim
+            )
+    return g_now
 
 
 def layer_norm(row_data, gain_vec, shift_vec):
@@ -143,9 +167,7 @@
     decode_out = decode_out.astype(jnp.bfloat16).reshape(decode_count, -1)
     attended = jnp.concatenate([prompt_out, decode_out], axis=0)
     mixed = jnp.dot(
-        attended,
-        lax.all_gather(output_weight, "req", axis=1, tiled=True),
-        preferred_element_type=jnp.float32,
+        attended, write_sites_in(output_weight, "req", 1), preferred_element_type=jnp.float32
     )
     summed = lax.psum_scatter(
         mixed.astype(jnp.bfloat16), "mp", scatter_dimension=1, tiled=True

time: 486 us -> 509 us (1.047)
  blocking collectives: 123 us -> 74.5 us
  starting transfers between devices: 17.3 us -> 44.3 us
  local copies, waits for them, and re-layouts: 71 us -> 92.3 us
  waiting for transfers between devices: 229 us -> 249 us
    unnamed x6 -> x5, waiting for transfers between devices: 79.3 us -> 132 us
    all_to_all x1 -> x0, blocking collectives: 48.4 us -> none  [on_device(): lax.all_to_all(normed, 'req', split_axis=1, concat_axis=0, tiled=True)]
    ppermute x0 -> x15, waiting for transfers between devices: none -> 39 us  [the longest x8 39 us: write_sites_in(): lax.ppermute(right_arr, mesh_name, [(dev_i, (dev_i + 1) % now) for dev_i...]
    all_gather x1 -> x0, waiting for transfers between devices: 36.3 us -> none  [on_device(): lax.all_gather(output_weight, 'req', axis=1, tiled=True)]
    dynamic_update_slice x0 -> x16, local copies, waits for them, and re-layouts: none -> 15.3 us  [the longest x8 7.15 us: write_sites_in(): lax.dynamic_update_slice_in_dim(g_now, right_arr, (outer - tick) % now *...]
    all_to_all x1, waiting for transfers between devices: 46.5 us -> 33.7 us  [on_device(): lax.all_to_all(outgoing, 'req', split_axis=0, concat_axis=0, tiled=True)]
    ppermute x0 -> x15, starting transfers between devices: none -> 12.6 us  [the longest x7 12.3 us: write_sites_in(): lax.ppermute(r1, mesh_name, [(dev_i, (dev_i - 1) % now) for dev_i in rang...]
    all_gather x1, waiting for transfers between devices: 54.4 us -> 44.5 us  [on_device(): gathered = lax.all_gather(tokens, 'mp', axis=1, tiled=True)]
  transfers between devices with their start and end apart: 7 -> 22, of which waited for: 6 -> 11; matrix products, arithmetic and copies ran while one was open for 14% -> 19% of each run, Pallas kernels for 0% -> 0%
where the time goes in v1:
time: 509 us; the launch traced here: 508 us
  waiting for transfers between devices  249 us (49%)
  local copies, waits for them, and re-layouts  92.3 us (18%)
  blocking collectives  74.5 us (15%)
  starting transfers between devices  44.3 us (9%)
  matrix products  20.4 us (4%)
  between operations  14.5 us (3%)
  other arithmetic  12.5 us (2%)
    unnamed x5, waiting for transfers between devices  132 us
    psum x1, blocking collectives, on_device(): reduced_rank_rows = lax.psum(reduced_rank_rows, 'mp').astype(jnp.bfloat16)  74.5 us
    all_gather x1, waiting for transfers between devices, on_device(): gathered = lax.all_gather(tokens, 'mp', axis=1, tiled=True)  44.5 us
    ppermute x8, waiting for transfers between devices, write_sites_in(): lax.ppermute(right_arr, mesh_name, [(dev_i, (dev_i + 1) % now) for dev_i...  39 us
    unnamed x40, local copies, waits for them, and re-layouts  38.3 us
    all_to_all x1, waiting for transfers between devices, on_device(): lax.all_to_all(outgoing, 'req', split_axis=0, concat_axis=0, tiled=True)  33.7 us
    slice x1, local copies, waits for them, and re-layouts, on_device(): cache[:, :, 0].reshape(decode_count, cache_len, head_count, HEAD_DIM)  13.8 us
    ppermute x7, starting transfers between devices, write_sites_in(): lax.ppermute(r1, mesh_name, [(dev_i, (dev_i - 1) % now) for dev_i in rang...  12.3 us
  transfers between devices with their start and end apart: 22, of which 11 were waited for; matrix products, arithmetic and copies ran while one was open for 19% of the time, Pallas kernels for 0%

profile of v1, /device:TPU:32, one launch (start us, length us, event | category | flops | bytes accessed | tf_op | source)
XLA Modules:
  0.0 507.8 jit_solution(14164889770790790078)
XLA Ops:
  8.6 8.6 %all-to-all-start.1 = ((s32[16,1,98]{2,1,0:T(1,128)}), s32[16,1,98]{2,1,0:T(1,128)S(1)}, u32[]{:S(2)}, u32[]{:S(2)}) async-start(s32[16,1,98]{2,1,0:T(1,128)} %compare_select_fusion), calls=%async_computation.1 | async-start | bytes 16384 | tf_op jit(solution)/shard_map/all_to_all | solution.py:94
  17.2 44.5 %all-gather.3.cloned.1.call-done = bf16[16,448,98]{1,2,0:T(8,128)(2,1)} async-done(((bf16[1,448,98]{1,2,0:T(8,128)(2,1)}), bf16[16,448,98]{1,2,0:T(8,128)(2,1)}) %all-gather.3.cloned.1.call-update) | async-done | bytes 1404944 | tf_op jit(solution)/shard_map/all_gather | solution.py:67
  61.7 3.8 copy.59
  65.5 4.6 reshape.248
  70.4 2.5 multiply_reduce_fusion
  76.2 7.5 %all-to-all-start.2 = ((bf16[16,98,448]{2,1,0:T(8,128)(2,1)}), bf16[16,98,448]{2,1,0:T(8,128)(2,1)}, u32[]{:S(2)}, u32[]{:S(2)}) async-start(bf16[16,98,448]{2,1,0:T(8,128)(2,1)} %broadcast_select_fusion), calls=%async_computation.2 | async-start | bytes 3407872 | tf_op jit(solution)/shard_map/all_to_all | solution.py:93
  83.7 3.2 all_to_all.24
  89.1 33.7 %all-to-all-done.2 = bf16[16,98,448]{2,1,0:T(8,128)(2,1)} async-done(((bf16[16,98,448]{2,1,0:T(8,128)(2,1)}), bf16[16,98,448]{2,1,0:T(8,128)(2,1)}, u32[]{:S(2)}, u32[]{:S(2)}) %all-to-all-start.2) | async-done | bytes 1404960 | tf_op jit(solution)/shard_map/all_to_all | solution.py:93
  122.7 6.6 %all-to-all-start = ((bf16[98,16,448]{2,0,1:T(8,128)(2,1)}), bf16[98,16,448]{2,0,1:T(8,128)(2,1)S(1)}, u32[]{:S(2)}, u32[]{:S(2)}) async-start(bf16[98,16,448]{2,0,1:T(8,128)(2,1)} %copy.60), calls=%async_computation | async-start | bytes 3407872 | tf_op jit(solution)/shard_map/all_to_all | solution.py:71
  131.1 2.2 fusion.10
  133.4 74.5 %all-reduce.5 = bf16[16,98,32]{1,2,0:T(8,128)(2,1)S(1)} all-reduce(f32[16,98,32]{1,2,0:T(8,128)S(1)} %fusion.10), channel_id=1, replica_groups=mesh['req'=16,'mp'=16] {'mp'}, use_global_device_ids=true, to_apply=%region_4.5 | all-reduce | flops 50176 | bytes 301056 | tf_op jit(solution)/shard_map/psum | solution.py:103
  208.8 3.9 copy.65
  213.9 8.7 %all-to-all-start.3 = ((bf16[16,98,2,384]{3,2,1,0:T(2,128)(2,1)}), bf16[16,98,2,384]{3,2,1,0:T(2,128)(2,1)S(1)}, u32[]{:S(2)}, u32[]{:S(2)}) async-start(bf16[16,98,2,384]{3,2,1,0:T(2,128)(2,1)} %copy.65), calls=%async_computation.3 | async-start | bytes 4816896 | tf_op jit(solution)/shard_map/all_to_all | solution.py:113
  222.6 2.9 all_to_all.27
  225.5 6.6 %fusion.5 = f32[1568,3,384]{2,0,1:T(8,128)} fusion(bf16[3,448,384]{2,1,0:T(8,128)(2,1)S(1)} %copy-done, bf16[1568,448]{1,0:T(8,128)(2,1)} %all_to_all.27), kind=kOutput, calls=%fused_computation.11 | convolution fusion | flops 1618477056 | bytes 9662464 | tf_op jit(solution)/shard_map/rd,cde->rce/dot_general | solution.py:73
  232.4 13.8 %fusion.54 = (bf16[2,2048,1,384]{3,2,1,0:T(2,128)(2,1)}, bf16[2,2048,1,384]{3,2,1,0:T(2,128)(2,1)}) fusion(bf16[2,2048,2,384]{3,2,1,0:T(2,128)(2,1)} %param.22), kind=kLoop, calls=%fused_computation.119 | loop fusion | bytes 12582912 | tf_op jit(solution)/shard_map/slice | solution.py:143
  248.3 15.4 %copy.100 = bf16[2,2048,1,384]{1,3,0,2:T(8,128)(2,1)} copy(bf16[2,2048,1,384]{3,2,1,0:T(2,128)(2,1)} %get-tuple-element.9) | data formatting | bytes 6291456
  263.7 15.4 %copy.101 = bf16[2,2048,1,384]{1,3,0,2:T(8,128)(2,1)} copy(bf16[2,2048,1,384]{3,2,1,0:T(2,128)(2,1)} %get-tuple-element.10) | data formatting | bytes 6291456
  280.4 11.9 %collective-permute-done.2 = bf16[384,448]{0,1:T(8,128)(2,1)S(1)} collective-permute-done((bf16[384,448]{0,1:T(8,128)(2,1)}, bf16[384,448]{0,1:T(8,128)(2,1)S(1)}, u32[]{:S(2)}, u32[]{:S(2)}) %collective-permute-start.2) | collective-permute-done | bytes 344096 | tf_op jit(solution)/shard_map/ppermute | solution.py:20
  294.5 2.8 broadcast_in_dim.145
  299.1 3.5 collective-permute-done.4
  307.9 5.0 collective-permute-done.6
  316.9 6.2 %collective-permute-done.8 = bf16[384,448]{0,1:T(8,128)(2,1)S(1)} collective-permute-done((bf16[384,448]{0,1:T(8,128)(2,1)S(1)}, bf16[384,448]{0,1:T(8,128)(2,1)S(1)}, u32[]{:S(2)}, u32[]{:S(2)}) %collective-permute-start.8) | collective-permute-done | bytes 344096 | tf_op jit(solution)/shard_map/ppermute | solution.py:20
  327.2 5.4 %collective-permute-done.10 = bf16[384,448]{0,1:T(8,128)(2,1)S(1)} collective-permute-done((bf16[384,448]{0,1:T(8,128)(2,1)S(1)}, bf16[384,448]{0,1:T(8,128)(2,1)S(1)}, u32[]{:S(2)}, u32[]{:S(2)}) %collective-permute-start.10) | collective-permute-done | bytes 344096 | tf_op jit(solution)/shard_map/ppermute | solution.py:20
  336.7 2.6 collective-permute-done.12
  341.6 4.4 collective-permute-done.14
  346.7 50.8 %all-reduce.4.cloned.1.call-done = f32[1568,3,384]{2,0,1:T(8,128)} async-done(((f32[1568,3,384]{2,0,1:T(8,128)}), f32[1568,3,384]{2,0,1:T(8,128)}) %all-reduce.4.cloned.1.call-update) | async-done | bytes 7225360
  404.8 2.4 fusion.43
  407.8 2.8 fusion.34
  411.4 5.0 convolution_convert_fusion
  416.4 2.4 copy.98
  418.8 80.8 %reduce-scatter.5.cloned.1.call-done = bf16[448,98]{1,0:T(8,128)(2,1)} async-done(((bf16[7168,98]{1,0:T(8,128)(2,1)}), bf16[448,98]{1,0:T(8,128)(2,1)}) %reduce-scatter.5.cloned.1.call-update) | async-done | bytes 87824
  (130 shorter events, 49.1 us)
Async XLA Ops:
  6.5 218.9 %copy-start = (bf16[3,448,384]{2,1,0:T(8,128)(2,1)S(1)}, bf16[3,448,384]{2,1,0:T(8,128)(2,1)}, u32[]{:S(2)}) copy-start(bf16[3,448,384]{2,1,0:T(8,128)(2,1)} %param.16) | copy-start | bytes 3096580
  6.5 55.1 %all-gather.3.cloned.1.call-start = ((), (), s32[]{:S(2)}) async-start(), calls=%async_computation.5 | async-start | bytes 1810432 | tf_op jit(solution)/shard_map/all_gather | solution.py:67
  8.6 67.6 %all-to-all-start.1 = ((s32[16,1,98]{2,1,0:T(1,128)}), s32[16,1,98]{2,1,0:T(1,128)S(1)}, u32[]{:S(2)}, u32[]{:S(2)}) async-start(s32[16,1,98]{2,1,0:T(1,128)} %compare_select_fusion), calls=%async_computation.1 | async-start | bytes 16384 | tf_op jit(solution)/shard_map/all_to_all | solution.py:94
  76.2 46.5 %all-to-all-start.2 = ((bf16[16,98,448]{2,1,0:T(8,128)(2,1)}), bf16[16,98,448]{2,1,0:T(8,128)(2,1)}, u32[]{:S(2)}, u32[]{:S(2)}) async-start(bf16[16,98,448]{2,1,0:T(8,128)(2,1)} %broadcast_select_fusion), calls=%async_computation.2 | async-start | bytes 3407872 | tf_op jit(solution)/shard_map/all_to_all | solution.py:93
  83.7 47.4 %copy-start.13 = (bf16[4,448,32]{1,2,0:T(8,128)(2,1)S(1)}, bf16[4,448,32]{1,2,0:T(8,128)(2,1)}, u32[]{:S(2)}) copy-start(bf16[4,448,32]{1,2,0:T(8,128)(2,1)} %param.18) | copy-start | bytes 344068
  87.0 120.9 %copy-start.7 = (bf16[4,2,16,384]{3,2,1,0:T(8,128)(2,1)S(1)}, bf16[4,2,16,384]{3,2,1,0:T(8,128)(2,1)}, u32[]{:S(2)}) copy-start(bf16[4,2,16,384]{3,2,1,0:T(8,128)(2,1)} %param.19) | copy-start | bytes 294916
  122.7 89.9 %all-to-all-start = ((bf16[98,16,448]{2,0,1:T(8,128)(2,1)}), bf16[98,16,448]{2,0,1:T(8,128)(2,1)S(1)}, u32[]{:S(2)}, u32[]{:S(2)}) async-start(bf16[98,16,448]{2,0,1:T(8,128)(2,1)} %copy.60), calls=%async_computation | async-start | bytes 3407872 | tf_op jit(solution)/shard_map/all_to_all | solution.py:71
  129.4 116.8 %collective-permute-start = (bf16[384,448]{0,1:T(8,128)(2,1)}, bf16[384,448]{0,1:T(8,128)(2,1)}, u32[]{:S(2)}, u32[]{:S(2)}) collective-permute-start(bf16[384,448]{0,1:T(8,128)(2,1)} %param.24), channel_id=1, source_target_pairs={{0,16},{16,32},{32,48},{48,64},{64,80},{80,96},{96,112},{112,128},... | collective-permute-start | bytes 1032200 | tf_op jit(solution)/shard_map/ppermute | solution.py:20
  129.5 116.8 %collective-permute-start.1 = (bf16[384,448]{0,1:T(8,128)(2,1)}, bf16[384,448]{0,1:T(8,128)(2,1)}, u32[]{:S(2)}, u32[]{:S(2)}) collective-permute-start(bf16[384,448]{0,1:T(8,128)(2,1)} %param.24), channel_id=1, source_target_pairs={{0,240},{16,0},{32,16},{48,32},{64,48},{80,64},{96,80},{112,96},{1... | collective-permute-start | bytes 1032200 | tf_op jit(solution)/shard_map/ppermute | solution.py:27
  213.9 186.3 %all-to-all-start.3 = ((bf16[16,98,2,384]{3,2,1,0:T(2,128)(2,1)}), bf16[16,98,2,384]{3,2,1,0:T(2,128)(2,1)S(1)}, u32[]{:S(2)}, u32[]{:S(2)}) async-start(bf16[16,98,2,384]{3,2,1,0:T(2,128)(2,1)} %copy.65), calls=%async_computation.3 | async-start | bytes 4816896 | tf_op jit(solution)/shard_map/all_to_all | solution.py:113
  222.5 175.0 %all-reduce.4.cloned.1.call-start = ((), (), s32[]{:S(2)}) async-start(), calls=%async_computation.7 | async-start | bytes 14450688
  232.1 15.8 %copy-start.12 = (s32[2]{0:T(128)S(1)}, s32[2]{0:T(128)}, u32[]{:S(2)}) copy-start(s32[2]{0:T(128)} %param.23) | copy-start | bytes 28
  232.2 267.4 %reduce-scatter.5.cloned.1.call-start = ((), (), s32[]{:S(2)}) async-start(), calls=%async_computation.6 | async-start | bytes 1949696
  246.2 46.2 %collective-permute-start.2 = (bf16[384,448]{0,1:T(8,128)(2,1)}, bf16[384,448]{0,1:T(8,128)(2,1)S(1)}, u32[]{:S(2)}, u32[]{:S(2)}) collective-permute-start(bf16[384,448]{0,1:T(8,128)(2,1)} %collective-permute-done), channel_id=1, source_target_pairs={{0,16},{16,32},{32,48},{48,64},{64,80},{80,96},{96,112},{112,128},... | collective-permute-start | bytes 1032200 | tf_op jit(solution)/shard_map/ppermute | solution.py:20
  246.3 46.1 %collective-permute-start.3 = (bf16[384,448]{0,1:T(8,128)(2,1)}, bf16[384,448]{0,1:T(8,128)(2,1)S(1)}, u32[]{:S(2)}, u32[]{:S(2)}) collective-permute-start(bf16[384,448]{0,1:T(8,128)(2,1)} %collective-permute-done.1), channel_id=1, source_target_pairs={{0,240},{16,0},{32,16},{48,32},{64,48},{80,64},{96,80},{112,96},{1... | collective-permute-start | bytes 1032200 | tf_op jit(solution)/shard_map/ppermute | solution.py:27
  263.7 15.4 %copy-start.15 = (u32[256]{0:T(256)S(1)}, u32[256]{0:T(256)}, u32[]{:S(2)}) copy-start(u32[256]{0:T(256)} %constant.172) | copy-start | bytes 3076
  263.7 28.7 %copy-start.14 = (s32[3]{0:T(128)S(1)}, s32[3]{0:T(128)}, u32[]{:S(2)}) copy-start(s32[3]{0:T(128)} %param.21) | copy-start | bytes 40
  292.3 10.3 %collective-permute-start.4 = (bf16[384,448]{0,1:T(8,128)(2,1)S(1)}, bf16[384,448]{0,1:T(8,128)(2,1)S(1)}, u32[]{:S(2)}, u32[]{:S(2)}) collective-permute-start(bf16[384,448]{0,1:T(8,128)(2,1)S(1)} %collective-permute-done.2), channel_id=1, source_target_pairs={{0,16},{16,32},{32,48},{48,64},{64,80},{80,96},{96,112},{112,128},... | collective-permute-start | bytes 1032200 | tf_op jit(solution)/shard_map/ppermute | solution.py:20
  292.4 12.0 %collective-permute-start.5 = (bf16[384,448]{0,1:T(8,128)(2,1)S(1)}, bf16[384,448]{0,1:T(8,128)(2,1)S(1)}, u32[]{:S(2)}, u32[]{:S(2)}) collective-permute-start(bf16[384,448]{0,1:T(8,128)(2,1)S(1)} %collective-permute-done.3), channel_id=1, source_target_pairs={{0,240},{16,0},{32,16},{48,32},{64,48},{80,64},{96,80},{112,96},{1... | collective-permute-start | bytes 1032200 | tf_op jit(solution)/shard_map/ppermute | solution.py:27
  302.6 10.2 %collective-permute-start.6 = (bf16[384,448]{0,1:T(8,128)(2,1)S(1)}, bf16[384,448]{0,1:T(8,128)(2,1)S(1)}, u32[]{:S(2)}, u32[]{:S(2)}) collective-permute-start(bf16[384,448]{0,1:T(8,128)(2,1)S(1)} %collective-permute-done.4), channel_id=1, source_target_pairs={{0,16},{16,32},{32,48},{48,64},{64,80},{80,96},{96,112},{112,128},... | collective-permute-start | bytes 1032200 | tf_op jit(solution)/shard_map/ppermute | solution.py:20
  302.6 96.0 %copy-start.10 = (f32[3,384]{1,0:T(4,128)S(1)}, f32[3,384]{1,0:T(4,128)}, u32[]{:S(2)}) copy-start(f32[3,384]{1,0:T(4,128)} %param.17) | copy-start | bytes 13828
  304.4 10.0 %collective-permute-start.7 = (bf16[384,448]{0,1:T(8,128)(2,1)S(1)}, bf16[384,448]{0,1:T(8,128)(2,1)S(1)}, u32[]{:S(2)}, u32[]{:S(2)}) collective-permute-start(bf16[384,448]{0,1:T(8,128)(2,1)S(1)} %collective-permute-done.5), channel_id=1, source_target_pairs={{0,240},{16,0},{32,16},{48,32},{64,48},{80,64},{96,80},{112,96},{1... | collective-permute-start | bytes 1032200 | tf_op jit(solution)/shard_map/ppermute | solution.py:27
  312.8 10.3 %collective-permute-start.8 = (bf16[384,448]{0,1:T(8,128)(2,1)S(1)}, bf16[384,448]{0,1:T(8,128)(2,1)S(1)}, u32[]{:S(2)}, u32[]{:S(2)}) collective-permute-start(bf16[384,448]{0,1:T(8,128)(2,1)S(1)} %collective-permute-done.6), channel_id=1, source_target_pairs={{0,16},{16,32},{32,48},{48,64},{64,80},{80,96},{96,112},{112,128},... | collective-permute-start | bytes 1032200 | tf_op jit(solution)/shard_map/ppermute | solution.py:20
  314.4 10.3 %collective-permute-start.9 = (bf16[384,448]{0,1:T(8,128)(2,1)S(1)}, bf16[384,448]{0,1:T(8,128)(2,1)S(1)}, u32[]{:S(2)}, u32[]{:S(2)}) collective-permute-start(bf16[384,448]{0,1:T(8,128)(2,1)S(1)} %collective-permute-done.7), channel_id=1, source_target_pairs={{0,240},{16,0},{32,16},{48,32},{64,48},{80,64},{96,80},{112,96},{1... | collective-permute-start | bytes 1032200 | tf_op jit(solution)/shard_map/ppermute | solution.py:27
  323.2 9.5 %collective-permute-start.10 = (bf16[384,448]{0,1:T(8,128)(2,1)S(1)}, bf16[384,448]{0,1:T(8,128)(2,1)S(1)}, u32[]{:S(2)}, u32[]{:S(2)}) collective-permute-start(bf16[384,448]{0,1:T(8,128)(2,1)S(1)} %collective-permute-done.8), channel_id=1, source_target_pairs={{0,16},{16,32},{32,48},{48,64},{64,80},{80,96},{96,112},{112,128},... | collective-permute-start | bytes 1032200 | tf_op jit(solution)/shard_map/ppermute | solution.py:20
  324.7 9.5 %collective-permute-start.11 = (bf16[384,448]{0,1:T(8,128)(2,1)S(1)}, bf16[384,448]{0,1:T(8,128)(2,1)S(1)}, u32[]{:S(2)}, u32[]{:S(2)}) collective-permute-start(bf16[384,448]{0,1:T(8,128)(2,1)S(1)} %collective-permute-done.9), channel_id=1, source_target_pairs={{0,240},{16,0},{32,16},{48,32},{64,48},{80,64},{96,80},{112,96},{1... | collective-permute-start | bytes 1032200 | tf_op jit(solution)/shard_map/ppermute | solution.py:27
  332.6 6.7 %collective-permute-start.12 = (bf16[384,448]{0,1:T(8,128)(2,1)S(1)}, bf16[384,448]{0,1:T(8,128)(2,1)S(1)}, u32[]{:S(2)}, u32[]{:S(2)}) collective-permute-start(bf16[384,448]{0,1:T(8,128)(2,1)S(1)} %collective-permute-done.10), channel_id=1, source_target_pairs={{0,16},{16,32},{32,48},{48,64},{64,80},{80,96},{96,112},{112,128},... | collective-permute-start | bytes 1032200 | tf_op jit(solution)/shard_map/ppermute | solution.py:20
  334.2 6.7 %collective-permute-start.13 = (bf16[384,448]{0,1:T(8,128)(2,1)S(1)}, bf16[384,448]{0,1:T(8,128)(2,1)S(1)}, u32[]{:S(2)}, u32[]{:S(2)}) collective-permute-start(bf16[384,448]{0,1:T(8,128)(2,1)S(1)} %collective-permute-done.11), channel_id=1, source_target_pairs={{0,240},{16,0},{32,16},{48,32},{64,48},{80,64},{96,80},{112,96},{1... | collective-permute-start | bytes 1032200 | tf_op jit(solution)/shard_map/ppermute | solution.py:27
  339.3 6.7 %collective-permute-start.14 = (bf16[384,448]{0,1:T(8,128)(2,1)S(1)}, bf16[384,448]{0,1:T(8,128)(2,1)S(1)}, u32[]{:S(2)}, u32[]{:S(2)}) collective-permute-start(bf16[384,448]{0,1:T(8,128)(2,1)S(1)} %collective-permute-done.12), channel_id=1, source_target_pairs={{0,16},{16,32},{32,48},{48,64},{64,80},{80,96},{96,112},{112,128},... | collective-permute-start | bytes 1032200 | tf_op jit(solution)/shard_map/ppermute | solution.py:20
  411.3 90.0 %copy-start.1 = (bf16[3,448,384]{2,1,0:T(8,128)(2,1)S(1)}, bf16[3,448,384]{2,1,0:T(8,128)(2,1)}, u32[]{:S(2)}) copy-start(bf16[3,448,384]{2,1,0:T(8,128)(2,1)} %param.16) | copy-start | bytes 3096580
  411.4 89.3 %copy-start.6 = (bf16[98,448]{1,0:T(8,128)(2,1)S(1)}, bf16[98,448]{1,0:T(8,128)(2,1)}, u32[]{:S(2)}) copy-start(bf16[98,448]{1,0:T(8,128)(2,1)} %param.13) | copy-start | bytes 263428
  411.4 89.2 %copy-start.11 = (f32[448]{0:T(512)S(1)}, f32[448]{0:T(512)}, u32[]{:S(2)}) copy-start(f32[448]{0:T(512)} %param.25) | copy-start | bytes 5380
  (6 other events, 28.5 us)
Sparse Core Ops, SparseCore 0:
  9.8 51.8 all-gather.2
  232.3 165.2 all-reduce.3
  418.9 80.6 reduce-scatter.4
